TPU v7x, 32 devices: a whole 2x2x4 slice. The times are simulated.
32 devices in a mesh: gz: 8 (over z, x), gy: 4 (over y, core).
Axes of the slice: x: 2, y: 2, z: 4, core: 2. Of those that a mesh axis runs over, the one named last changes fastest.
Arguments:
- parcel_cell: int32 [131072], P(('gz', 'gy')), may hold values from 0 to 131071
- parcel_offset: float32 [3, 131072], P(None, ('gz', 'gy')), may hold values from 0 to 1
- parcel_volume: float32 [131072], P(('gz', 'gy')), may hold values from 1 to 8
- parcel_force: float32 [3, 131072], P(None, ('gz', 'gy')), may hold values from -24 to 24
- brick_counts: int32 [8, 4], P('gz', 'gy'), may hold values from 1 to 4096, as said below
- divergence: float32 [64, 256, 256], P('gz', 'gy'), may hold values from -6 to 6
- pressure_prev: float32 [64, 256, 256], P('gz', 'gy'), may hold values from -6 to 6
- gas_density: float32 [64, 256, 256], P('gz', 'gy'), may hold values from 0.5 to 2
Outputs:
- gas_fraction: float32 [64, 256, 256], P('gz', 'gy')
- momentum_source: float32 [64, 3, 256, 256], P('gz', None, 'gy')
- pressure: float32 [64, 256, 256], P('gz', 'gy')
- residual: float32 [64, 256, 256], P('gz', 'gy')
Inputs may be any that keep to these rules, and one draw needn't show every extreme that they name: brick_counts gives the number of live parcels of each brick, held in the brick's first slots; one brick holds exactly 4096 and one exactly 1.
All inputs are finite; a program needn't handle non-finite values.
Results may differ from a plain program's by a relative error of at most 0.0021.
Values sent between devices are 32-bit elements; how exact they have to be, the bound alone decides.
A program may use at most 64 MiB of HBM per device.

v0:
```python
import functools
import math

import jax
import jax.numpy as jnp
from jax import lax
from jax.experimental import pallas as pl
from jax.experimental.pallas import tpu as pltpu
from jax.sharding import PartitionSpec as P

SWEEPS = 3
REACH = 3
HALO = SWEEPS + 1
EDGE = 2 * HALO
CHUNK = 1024
LANES = 128
smooth_rate = 0.15
stiffness = 0.002
F32 = jnp.float32
MESH = pl.DeviceIdType.MESH


def tap(distance):
    return jnp.exp2((-0.5 * math.log2(math.e)) * (distance * distance))


def split_cell(cell, ny, nx):
    if ny & (ny - 1) == 0 and nx & (nx - 1) == 0:
        sx, sy = nx.bit_length() - 1, ny.bit_length() - 1
        return (
            lax.shift_right_logical(cell, sx + sy),
            lax.shift_right_logical(cell, sx) & (ny - 1),
            cell & (nx - 1),
        )
    row = lax.div(cell, nx)
    return lax.div(row, ny), lax.rem(row, ny), lax.rem(cell, nx)


def step_kernel(
    ngz, ngy, nz, ny, nx, slots,
    count_ref, cell_hbm, off_hbm, vol_hbm, force_hbm, div_hbm, p_hbm, den_hbm,
    gf_ref, mom_ref, out_ref, res_ref,
    cell_ref, off_ref, vol_ref, force_ref, div_ref, p_ref, den_ref, pk_ref, near, wz_ref, wy_ref, wx_ref, dep, fld, tile_in,
    halo_z, halo_y, edge, edge_in, mob, face_z, face_s, face_n, face_w, face_e, diag,
    r_ref, z_ref, q_ref, w_ref, aw_ref, row_ref, red,
    load_sem, near_send, near_recv, tile_send, tile_recv, hz_send, hz_recv, hy_send, hy_recv,
    row_send, row_recv,
):
    gz, gy = lax.axis_index("gz"), lax.axis_index("gy")
    planes, rows = nz + 2 * HALO, ny + EDGE
    total_y = ngy * ny
    first = gy * ny
    count = ngz * ngy
    me = gz * ngy + gy
    odd = lax.rem(gz, 2)
    up, down = lax.rem(gz + 1, ngz), lax.rem(gz + ngz - 1, ngz)
    partner, other = jnp.where(odd == 1, down, up), jnp.where(odd == 1, up, down)
    north_gy, south_gy = lax.rem(gy + 1, ngy), lax.rem(gy + ngy - 1, ngy)
    has_s, has_n = gy > 0, gy < ngy - 1

    loads = [
        pltpu.make_async_copy(src, dst, load_sem.at[n])
        for n, (src, dst) in enumerate((
            (cell_hbm, cell_ref), (off_hbm, off_ref), (vol_hbm, vol_ref), (force_hbm, force_ref),
            (den_hbm, den_ref), (p_hbm, p_ref), (div_hbm, div_ref),
        ))
    ]
    for c in loads:
        c.start()

    def place_of(d):
        to = lax.rem(me + d, count)
        to_z = lax.div(to, ngy)
        return {"gz": to_z, "gy": to - to_z * ngy}

    def each_other(body):
        if count <= 64:
            for d in range(1, count):
                body(d)
        else:
            lax.fori_loop(1, count, lambda d, carry: (body(d), carry)[1], 0)

    barrier = pltpu.get_barrier_semaphore()
    each_other(lambda d: pl.semaphore_signal(barrier, inc=1, device_id=place_of(d), device_id_type=MESH))

    for c in loads[:4]:
        c.wait()
    live = lax.broadcasted_iota(jnp.int32, (1, slots), 1) < count_ref[0, 0]
    volume = jnp.where(live, vol_ref[...], 0.0)
    pk_ref[0:1] = volume
    pk_ref[1:4] = volume * force_ref[...]
    pk_ref[4:5] = cell_ref[...].astype(F32)
    pk_ref[5:8] = off_ref[...]

    def remote(src, dst, send, recv, where):
        return pltpu.make_async_remote_copy(
            src_ref=src, dst_ref=dst, send_sem=send, recv_sem=recv, device_id=where, device_id_type=MESH
        )

    near_copies = [
        remote(pk_ref, near.at[n], near_send.at[n], near_recv.at[n], {"gz": to}) for n, to in enumerate((partner, other))
    ]

    def pair_z(slot, src):
        far_plane, far_side = odd * (nz - 1), 1 - odd
        near_plane, near_side = (1 - odd) * (nz - 1), odd
        return [
            remote(src.at[far_plane], halo_z.at[slot, far_side], hz_send.at[slot, 0], hz_recv.at[slot, 0], {"gz": other}),
            remote(
                src.at[near_plane], halo_z.at[slot, near_side], hz_send.at[slot, 1], hz_recv.at[slot, 1], {"gz": partner}
            ),
        ]

    def pair_y(slot, to_north, to_south, from_south, from_north):
        return (
            remote(to_north, from_south, hy_send.at[slot, 0], hy_recv.at[slot, 0], {"gy": north_gy}),
            remote(to_south, from_north, hy_send.at[slot, 1], hy_recv.at[slot, 1], {"gy": south_gy}),
        )

    def start_y(pair):
        north, south = pair

        @pl.when(has_n)
        def _():
            north.start()

        @pl.when(has_s)
        def _():
            south.start()

    def wait_y(pair):
        north, south = pair

        @pl.when(has_n)
        def _():
            north.wait_send()
            south.wait_recv()

        @pl.when(has_s)
        def _():
            south.wait_send()
            north.wait_recv()

    def start_z(pair):
        for c in pair:
            c.start()

    def wait_z(pair):
        for c in pair:
            c.wait()

    def tile_pair(slot, src):
        return pair_y(
            slot, src.at[:, pl.ds(ny - 8, 8), :], src.at[:, pl.ds(0, 8), :], halo_y.at[slot, 0], halo_y.at[slot, 1]
        )

    p_z, den_z, p_y, den_y = pair_z(0, p_ref), pair_z(1, den_ref), tile_pair(0, p_ref), tile_pair(1, den_ref)

    iota8 = lax.broadcasted_iota(jnp.int32, (8, LANES), 0).astype(F32)
    iota16 = lax.broadcasted_iota(jnp.int32, (16, LANES), 0).astype(F32)
    plane_id = (lax.broadcasted_iota(jnp.int32, (planes, LANES), 0) - HALO).astype(F32)
    south_end = jnp.where(has_s, 0, HALO).astype(F32)
    north_end = jnp.where(has_n, rows, rows - HALO).astype(F32)

    def masked(t, half):
        return jnp.where(jnp.abs(t) <= REACH, tap(t + half), 0.0)

    def split_blocks(home, size):
        block = jnp.floor(home * (1.0 / size))
        inner = home - block * size
        low = inner < size // 2
        return block, inner, jnp.where(low, block - 1.0, block + 1.0), jnp.where(low, -1.0 * size, 1.0 * size)

    def prepare(pk, brick, slot, at, width):
        for off in range(0, width, LANES):
            sl = pl.ds(pl.multiple_of(at + off, LANES), LANES)
            cz, cy, cx = [c.astype(F32) for c in split_cell(pk[4:5, sl].astype(jnp.int32), ny, nx)]
            hz, hy, hx = 0.5 - pk[5:6, sl], 0.5 - pk[6:7, sl], 0.5 - pk[7:8, sl]
            sum_z = jnp.sum(masked(iota8 - REACH, hz), axis=0, keepdims=True)
            wz_ref[slot, :, sl] = masked(plane_id - (cz + brick), hz) * (1.0 / sum_z)

            block, inner, beside, shift = split_blocks(cy + HALO, 8)
            t0 = iota8 - inner
            t1 = t0 + shift
            r0 = iota8 + block * 8
            r1 = iota8 + beside * 8
            v0 = jnp.where((r0 >= south_end) & (r0 < north_end), masked(t0, hy), 0.0)
            v1 = jnp.where((r1 >= south_end) & (r1 < north_end), masked(t1, hy), 0.0)
            scale = 1.0 / jnp.sum(v0 + v1, axis=0, keepdims=True)
            v0, v1 = v0 * scale, v1 * scale
            block, beside = jnp.broadcast_to(block, (8, LANES)), jnp.broadcast_to(beside, (8, LANES))
            for g in range(rows // 8):
                wy_ref[slot, 8 * g : 8 * g + 8, sl] = jnp.where(block == g, v0, jnp.where(beside == g, v1, 0.0))

            block, inner, beside, shift = split_blocks(cx, 16)
            t0 = iota16 - inner
            t1 = t0 + shift
            inside = (beside >= 0) & (beside < nx // 16)
            v0 = masked(t0, hx)
            v1 = jnp.where(inside, masked(t1, hx), 0.0)
            scale = 1.0 / jnp.sum(v0 + v1, axis=0, keepdims=True)
            v0, v1 = (v0 * scale).astype(jnp.bfloat16), (v1 * scale).astype(jnp.bfloat16)
            block = jnp.broadcast_to(block, (16, LANES)).astype(jnp.bfloat16)
            beside = jnp.broadcast_to(beside, (16, LANES)).astype(jnp.bfloat16)
            none = jnp.zeros((16, LANES), jnp.bfloat16)
            for g in range(nx // 16):
                wx_ref[slot, 16 * g : 16 * g + 16, sl] = jnp.where(block == g, v0, jnp.where(beside == g, v1, none))

    def deposit(pk, slot, lo, n, add, beside=None, after=None):
        def body(j, carry):
            i = lo + j
            acc = None
            for at in range(0, slots, CHUNK):
                sl = pl.ds(at, CHUNK)
                scaled = pk[0:4, sl] * wz_ref[slot, pl.ds(i, 1), sl]
                wy = wy_ref[slot, :, sl]
                lhs = jnp.concatenate([scaled[k : k + 1] * wy for k in range(4)], axis=0).astype(jnp.bfloat16)
                part = lax.dot_general(
                    lhs, wx_ref[slot, :, sl], (((1,), (1,)), ((), ())), preferred_element_type=F32
                )
                acc = part if acc is None else acc + part
                if beside is not None:
                    beside(j * (slots // CHUNK) + at // CHUNK)
            acc = acc.reshape(4, rows, nx)
            dep[i] = dep[i] + acc if add else acc
            if after is not None:
                after(i)
            return carry

        lax.fori_loop(0, n, body, 0)

    dep[0] = jnp.zeros((4, rows, nx), F32)
    dep[planes - 1] = jnp.zeros((4, rows, nx), F32)

    def prepare_all(pk, brick, slot):
        def body(i, carry):
            prepare(pk, brick, slot, i * 4 * LANES, 4 * LANES)
            return carry

        lax.fori_loop(0, slots // (4 * LANES), body, 0)

    prepare_all(pk_ref, 0.0, 0)
    reach = HALO + REACH
    side = (1 - 2 * odd).astype(F32) * nz
    lo_near, lo_far = (1 - odd) * (planes - reach), odd * (planes - reach)
    ahead = planes - 2 * (HALO - REACH) - nz
    deposit(pk_ref, 0, HALO - REACH, ahead, False)
    pl.semaphore_wait(barrier, count - 1)
    for c in near_copies:
        c.start()
    for c in loads[4:]:
        c.wait()
    start_y(den_y)
    start_y(p_y)
    deposit(pk_ref, 0, HALO - REACH + ahead, nz, False)

    def tile_pair_of(i):
        return (
            remote(
                dep.at[i, :, pl.ds(ny, EDGE), :], tile_in.at[0, i], tile_send.at[i, 0], tile_recv.at[i, 0],
                {"gy": north_gy},
            ),
            remote(
                dep.at[i, :, pl.ds(0, EDGE), :], tile_in.at[1, i], tile_send.at[i, 1], tile_recv.at[i, 1],
                {"gy": south_gy},
            ),
        )

    def send_tiles(i):
        start_y(tile_pair_of(i))

    near_copies[0].wait()
    prepare_all(near.at[0], side, 1)
    for i in range(reach, planes - reach):
        send_tiles(i)
    deposit(near.at[0], 1, lo_near, reach - 4, True, None, send_tiles)
    near_copies[1].wait()
    start_z(den_z)
    start_z(p_z)
    share = slots // (4 * (slots // CHUNK))

    def prepare_far(n):
        prepare(near.at[1], -side, 2, n * share, share)

    deposit(near.at[0], 1, lo_near + reach - 4, 4, True, prepare_far, send_tiles)
    deposit(near.at[1], 2, lo_far, reach, True, None, send_tiles)

    def add_tiles(lo, n):
        def body(j, carry):
            i = lo + j
            wait_y(tile_pair_of(i))

            @pl.when(has_s)
            def _():
                dep[i, :, 0:EDGE, :] = dep[i, :, 0:EDGE, :] + tile_in[0, i]

            @pl.when(has_n)
            def _():
                dep[i, :, ny : ny + EDGE, :] = dep[i, :, ny : ny + EDGE, :] + tile_in[1, i]

            return carry

        lax.fori_loop(0, n, body, 0)

    def shifts_x(v):
        lane = lax.broadcasted_iota(jnp.int32, (v.shape[0], LANES), 1)
        parts = [v[:, at : at + LANES] for at in range(0, nx, LANES)]
        ups = [pltpu.roll(part, 1, 1) for part in parts]
        downs = [pltpu.roll(part, LANES - 1, 1) for part in parts]
        west = [jnp.where(lane == 0, ups[n - 1] if n else 0.0, u) for n, u in enumerate(ups)]
        east = [
            jnp.where(lane == LANES - 1, downs[n + 1] if n + 1 < len(parts) else 0.0, u) for n, u in enumerate(downs)
        ]
        return jnp.concatenate(west, axis=1), jnp.concatenate(east, axis=1)

    def sweep(src, dst, lo, n):
        place = lax.broadcasted_iota(jnp.int32, (rows, nx), 0) - HALO + first
        lane = lax.broadcasted_iota(jnp.int32, (rows, nx), 1)
        count = (
            2.0
            + (place >= 1).astype(F32)
            + (place < total_y - 1).astype(F32)
            + (lane >= 1).astype(F32)
            + (lane < nx - 1).astype(F32)
        )
        inside = (place >= 0) & (place < total_y)
        scale_c = jnp.where(inside, 1.0 - smooth_rate * count, 0.0)
        scale_n = jnp.where(inside, smooth_rate, 0.0)

        def body(j, carry):
            i = lo + j
            for k in range(4):
                c = src[i, k]
                west, east = shifts_x(c)
                beside = (
                    src[i - 1, k] + src[i + 1, k] + pltpu.roll(c, 1, 0) + pltpu.roll(c, rows - 1, 0) + west + east
                )
                dst[i, k] = scale_c * c + scale_n * beside
            return carry

        lax.fori_loop(0, n, body, 0)

    half = planes // 2 - 1
    bufs = [dep, fld]
    add_tiles(lo_near + (odd - 1) * (planes - 2 * reach), planes - reach)
    sweep(dep, fld, 1 + (1 - odd) * half, half)
    add_tiles(lo_far, reach)
    sweep(dep, fld, 1 + odd * half, half)
    for s in range(1, SWEEPS):
        sweep(bufs[s % 2], bufs[(s + 1) % 2], s + 1, planes - 2 * s - 2)
    f = bufs[SWEEPS % 2]

    def own(v, shift=0):
        return pltpu.roll(v, rows - HALO - shift, 0)[0:ny]

    wait_y(den_y)
    wait_y(p_y)
    wait_z(den_z)
    wait_z(p_z)
    for z in range(-1, nz + 1):
        g = own(1.0 / (1.0 + f[z + HALO, 0]))
        if 0 <= z < nz:
            gf_ref[z] = g
            for k in range(3):
                mom_ref[z, k] = own(f[z + HALO, k + 1])
            den = den_ref[z]
        else:
            den = halo_z[1, 0 if z < 0 else 1]
        mob[z + 1] = g / den

    own_row = lax.broadcasted_iota(jnp.int32, (ny, nx), 0)

    def shifts_y(v, south_row, north_row):
        south = jnp.where(own_row == 0, south_row, pltpu.roll(v, 1, 0))
        north = jnp.where(own_row == ny - 1, north_row, pltpu.roll(v, ny - 1, 0))
        return south, north

    def halo_rows(slot, z):
        if slot < 2:
            south, north = halo_y[slot, 0, z, 7:8, :], halo_y[slot, 1, z, 0:1, :]
        else:
            south, north = edge_in[slot - 2, 0, z : z + 1, :], edge_in[slot - 2, 1, z : z + 1, :]
        return jnp.where(has_s, south, 0.0), jnp.where(has_n, north, 0.0)

    def apply(v, slot, z):
        c = v[z]
        below = v[z - 1] if z > 0 else halo_z[slot, 0]
        above = v[z + 1] if z < nz - 1 else halo_z[slot, 1]
        south, north = shifts_y(c, *halo_rows(slot, z))
        west, east = shifts_x(c)
        coupled = (
            face_z[z] * below + face_z[z + 1] * above + face_s[z] * south + face_n[z] * north
            + face_w[z] * west + face_e[z] * east
        )
        return diag[z] * c - coupled

    def keep_edge(slot, z, v):
        edge[slot, 0, z : z + 1, :] = v[ny - 1 : ny]
        edge[slot, 1, z : z + 1, :] = v[0:1]

    def edge_pair(slot):
        return pair_y(
            slot, edge.at[slot - 2, 0], edge.at[slot - 2, 1], edge_in.at[slot - 2, 0], edge_in.at[slot - 2, 1]
        )

    for z in range(nz + 1):
        face_z[z] = 0.5 * (mob[z] + mob[z + 1])
    order = [0, nz - 1] + list(range(1, nz - 1))
    inner_first = list(range(1, nz - 1)) + [0, nz - 1]
    z_z, w_z, z_y, w_y = pair_z(2, z_ref), pair_z(3, w_ref), edge_pair(2), edge_pair(3)
    for z in order:
        m = mob[z + 1]
        gs = f[z + HALO, 0, HALO - 1 : HALO, :]
        gn = f[z + HALO, 0, HALO + ny : HALO + ny + 1, :]
        ms = jnp.where(has_s, 1.0 / (1.0 + gs) / halo_y[1, 0, z, 7:8, :], 0.0)
        mn = jnp.where(has_n, 1.0 / (1.0 + gn) / halo_y[1, 1, z, 0:1, :], 0.0)
        south, north = shifts_y(m, ms, mn)
        west, east = shifts_x(m)
        fs, fn, fw, fe = 0.5 * (m + south), 0.5 * (m + north), 0.5 * (m + west), 0.5 * (m + east)
        face_s[z], face_n[z], face_w[z], face_e[z] = fs, fn, fw, fe
        dg = stiffness * m + face_z[z] + face_z[z + 1] + fs + fn + fw + fe
        diag[z] = dg
        mz_d, mz_u = own(f[z + HALO - 1, 1]), own(f[z + HALO + 1, 1])
        my = f[z + HALO, 2]
        xw, xe = shifts_x(own(f[z + HALO, 3]))
        spread = 0.5 * (mz_u - mz_d) + 0.5 * (own(my, 1) - own(my, -1)) + 0.5 * (xe - xw)
        r0 = div_ref[z] - spread - apply(p_ref, 0, z)
        r_ref[z] = r0
        z0 = r0 / dg
        z_ref[z] = z0
        keep_edge(0, z, z0)
        if z == nz - 1:
            start_z(z_z)
    start_y(z_y)

    def fold(v):
        part = jnp.sum(v, axis=0, keepdims=True)
        out = part[:, 0:LANES]
        for at in range(LANES, nx, LANES):
            out = out + part[:, at : at + LANES]
        for step in (64, 32):
            out = out + pltpu.roll(out, step, 1)
        return out

    sums = [jnp.zeros((ny, nx), F32)] * 4
    wait_y(z_y)
    for z in inner_first:
        if z == 0:
            wait_z(z_z)
        q = apply(z_ref, 2, z)
        w = q / diag[z]
        q_ref[z] = q
        w_ref[z] = w
        keep_edge(1, z, w)
    start_z(w_z)
    start_y(w_y)
    for z in range(nz):
        sums[0] = sums[0] + r_ref[z] * z_ref[z]
        sums[1] = sums[1] + z_ref[z] * q_ref[z]
        sums[2] = sums[2] + q_ref[z] * w_ref[z]
    wait_y(w_y)
    for z in inner_first:
        if z == 0:
            wait_z(w_z)
        aw = apply(w_ref, 3, z)
        aw_ref[z] = aw
        sums[3] = sums[3] + w_ref[z] * aw
    quarter = lax.broadcasted_iota(jnp.int32, (1, LANES), 1) // 32
    line = fold(sums[3])
    for n in range(3):
        line = jnp.where(quarter == n, fold(sums[n]), line)
    row_ref[0] = line

    def row_copy(d):
        return remote(row_ref.at[0], red.at[me], row_send.at[d - 1], row_recv.at[me], place_of(d))

    def row_from(d):
        whom = lax.rem(me + count - d, count)
        return remote(row_ref.at[0], red.at[whom], row_send.at[d - 1], row_recv.at[whom], place_of(d))

    each_other(lambda d: row_copy(d).start())
    red[me] = line
    each_other(lambda d: row_copy(d).wait_send())
    each_other(lambda d: row_from(d).wait_recv())
    total = jnp.sum(red[...], axis=0)
    norm0, curve0, mix, square = [
        jnp.sum(jnp.where(quarter == n, total, 0.0), axis=1, keepdims=True) for n in range(4)
    ]
    step0 = norm0 / curve0
    norm1 = norm0 - 2.0 * step0 * curve0 + step0 * step0 * mix
    curve1 = curve0 - 2.0 * step0 * mix + step0 * step0 * square
    beta = norm1 / norm0
    step1 = norm1 / (curve1 - beta * norm1 / step0)
    along, back = step0 + step1 * (1.0 + beta), step0 * step1
    for z in range(nz):
        out_ref[z] = p_ref[z] + along * z_ref[z] - back * w_ref[z]
        res_ref[z] = r_ref[z] - along * q_ref[z] + back * aw_ref[z]


def pass_kernel(*refs):
    ins, outs, put = refs[0:4], refs[4:8], refs[8]
    ways = [pltpu.make_async_copy(ins[n], outs[n], put.at[n]) for n in range(4)]
    for c in ways:
        c.start()
    for c in ways:
        c.wait()


def on_device(ngz, ngy, parcel_cell, parcel_offset, parcel_volume, parcel_force, brick_counts,
              divergence, pressure_prev, gas_density):
    nz, ny, nx = divergence.shape
    slots = parcel_cell.shape[0]
    planes, rows = nz + 2 * HALO, ny + EDGE
    field = jax.ShapeDtypeStruct((nz, ny, nx), F32)
    own = pltpu.VMEM((nz, ny, nx), F32)
    dma = pltpu.SemaphoreType.DMA
    vmem = pl.BlockSpec(memory_space=pltpu.VMEM)
    hbm = pl.BlockSpec(memory_space=pl.ANY)
    shapes = (field, jax.ShapeDtypeStruct((nz, 3, ny, nx), F32), field, field)
    count = ngz * ngy
    made = pl.pallas_call(
        functools.partial(step_kernel, ngz, ngy, nz, ny, nx, slots),
        out_shape=tuple(pltpu.VMEM(shape.shape, F32) for shape in shapes),
        in_specs=[pl.BlockSpec(memory_space=pltpu.SMEM)] + [hbm] * 7,
        out_specs=(vmem,) * 4,
        scratch_shapes=[
            pltpu.VMEM((1, slots), jnp.int32), pltpu.VMEM((3, slots), F32),
            pltpu.VMEM((1, slots), F32), pltpu.VMEM((3, slots), F32),
            own, own, own,
            pltpu.VMEM((8, slots), F32),
            pltpu.VMEM((2, 8, slots), F32),
            pltpu.VMEM((3, planes, slots), F32),
            pltpu.VMEM((3, rows, slots), F32),
            pltpu.VMEM((3, nx, slots), jnp.bfloat16),
            pltpu.VMEM((planes, 4, rows, nx), F32),
            pltpu.VMEM((planes, 4, rows, nx), F32),
            pltpu.VMEM((2, planes, 4, EDGE, nx), F32),
            pltpu.VMEM((4, 2, ny, nx), F32),
            pltpu.VMEM((2, 2, nz, 8, nx), F32),
            pltpu.VMEM((2, 2, nz, nx), F32),
            pltpu.VMEM((2, 2, nz, nx), F32),
            pltpu.VMEM((nz + 2, ny, nx), F32),
            pltpu.VMEM((nz + 1, ny, nx), F32),
            own, own, own, own, own,
            own, own, own, own, own,
            pltpu.VMEM((1, 1, 128), F32),
            pltpu.VMEM((count, 1, 128), F32),
            dma((7,)), dma((2,)), dma((2,)),
            dma((planes, 2)), dma((planes, 2)),
            dma((4, 2)), dma((4, 2)), dma((4, 2)), dma((4, 2)),
            dma((count,)), dma((count,)),
        ],
        compiler_params=pltpu.CompilerParams(
            collective_id=0, has_side_effects=True, vmem_limit_bytes=48 * 1024 * 1024
        ),
    )(brick_counts, *[
        pltpu.with_memory_space_constraint(array, pltpu.HBM)
        for array in (
            parcel_cell[None, :], parcel_offset, parcel_volume[None, :], parcel_force,
            divergence, pressure_prev, gas_density,
        )
    ])
    return pl.pallas_call(
        pass_kernel,
        out_shape=shapes,
        in_specs=[vmem] * 4,
        out_specs=(hbm,) * 4,
        scratch_shapes=[dma((4,))],
    )(*[pltpu.with_memory_space_constraint(array, pltpu.VMEM) for array in made])


def solution(mesh):
    ngz, ngy = mesh.shape["gz"], mesh.shape["gy"]
    return jax.shard_map(
        functools.partial(on_device, ngz, ngy),
        mesh=mesh,
        in_specs=(
            P(("gz", "gy")),
            P(None, ("gz", "gy")),
            P(("gz", "gy")),
            P(None, ("gz", "gy")),
            P("gz", "gy"),
            P("gz", "gy", None),
            P("gz", "gy", None),
            P("gz", "gy", None),
        ),
        out_specs=(
            P("gz", "gy", None),
            P("gz", None, "gy", None),
            P("gz", "gy", None),
            P("gz", "gy", None),
        ),
        check_vma=False,
    )
```

profile of v0, /device:TPU:0, one launch (start us, length us, event | category | flops | bytes accessed | tf_op | source)
XLA Modules:
  0.0 61.2 jit_solution(5841609248124458976)
XLA Ops:
  1.3 58.3 %shard_map.111 = (f32[8,64,256]{2,1,0:T(8,128)S(1)}, f32[8,3,64,256]{3,2,1,0:T(8,128)S(1)}, f32[8,64,256]{2,1,0:T(8,128)S(1)}, f32[8,64,256]{2,1,0:T(8,128)S(1)}) custom-call(s32[1,1]{1,0:T(1,128)S(6)} %copy.12.count_ref, s32[1,4096]{1,0:T(1,128)} %bitcast.2, f32[3,4096]{1,0:T(4,128)} %off_hbm.1, f32[1,4096]{1,0:T(1,128)} %bitcast.3, f32[3,4096]{1,0:T(4,128)} %force_hbm.1, ...), custom_call_target="tpu_custom_call" | custom-call | tf_op jit(solution)/shard_map/pallas_call | solution.py:521
  59.5 1.7 %shard_map.112 = (f32[8,64,256]{2,1,0:T(8,128)}, f32[8,3,64,256]{3,2,1,0:T(8,128)}, f32[8,64,256]{2,1,0:T(8,128)}, f32[8,64,256]{2,1,0:T(8,128)}) custom-call(f32[8,64,256]{2,1,0:T(8,128)S(1)} %get-tuple-element.8.refs_0_, f32[8,3,64,256]{3,2,1,0:T(8,128)S(1)} %get-tuple-element.9.refs_1_, f32[8,64,256]{2,1,0:T(8,128)S(1)} %get-tuple-element.10.refs_2_, ...), custom_call_target="tpu_custom_call" | custom-call | tf_op jit(solution)/shard_map/pallas_call | solution.py:563
where the time goes:
time: 61.5 us; the launch traced here: 61.2 us
  Pallas kernels  59.9 us (97%)
  between operations  1.29 us (2%)
    pallas_call x1, Pallas kernels, on_device(): pl.pallas_call(functools.partial(step_kernel, ngz, ngy, nz, ny, nx, slots...  58.3 us
    pallas_call x1, Pallas kernels, on_device(): pl.pallas_call(pass_kernel, out_shape=shapes, in_specs=[vmem] * 4, out_sp...  1.69 us

commit v1 on v0

--- a/solution.py
+++ b/solution.py
@@ -14,6 +14,9 @@
 EDGE = 2 * HALO
 CHUNK = 1024
 LANES = 128
+OWN_WIDE = 2
+NEAR_WIDE = 2
+BESIDE = 4
 smooth_rate = 0.15
 stiffness = 0.002
 F32 = jnp.float32
@@ -206,28 +209,34 @@
             for g in range(nx // 16):
                 wx_ref[slot, 16 * g : 16 * g + 16, sl] = jnp.where(block == g, v0, jnp.where(beside == g, v1, none))
 
-    def deposit(pk, slot, lo, n, add, beside=None, after=None):
+    def deposit(pk, slot, lo, n, add, wide=1, beside=None, after=None, parts=4):
+        assert n % wide == 0
+
         def body(j, carry):
-            i = lo + j
+            i = lo + j * wide
             acc = None
             for at in range(0, slots, CHUNK):
                 sl = pl.ds(at, CHUNK)
-                scaled = pk[0:4, sl] * wz_ref[slot, pl.ds(i, 1), sl]
                 wy = wy_ref[slot, :, sl]
-                lhs = jnp.concatenate([scaled[k : k + 1] * wy for k in range(4)], axis=0).astype(jnp.bfloat16)
+                stack = []
+                for h in range(wide):
+                    scaled = pk[0:parts, sl] * wz_ref[slot, pl.ds(i + h, 1), sl]
+                    stack += [scaled[k : k + 1] * wy for k in range(parts)]
+                lhs = jnp.concatenate(stack, axis=0).astype(jnp.bfloat16)
                 part = lax.dot_general(
                     lhs, wx_ref[slot, :, sl], (((1,), (1,)), ((), ())), preferred_element_type=F32
                 )
                 acc = part if acc is None else acc + part
                 if beside is not None:
                     beside(j * (slots // CHUNK) + at // CHUNK)
-            acc = acc.reshape(4, rows, nx)
-            dep[i] = dep[i] + acc if add else acc
-            if after is not None:
-                after(i)
+            acc = acc.reshape(wide, parts, rows, nx)
+            for h in range(wide):
+                dep[i + h, 0:parts] = dep[i + h, 0:parts] + acc[h] if add else acc[h]
+                if after is not None:
+                    after(i + h)
             return carry
 
-        lax.fori_loop(0, n, body, 0)
+        lax.fori_loop(0, n // wide, body, 0)
 
     dep[0] = jnp.zeros((4, rows, nx), F32)
     dep[planes - 1] = jnp.zeros((4, rows, nx), F32)
@@ -243,8 +252,10 @@
     reach = HALO + REACH
     side = (1 - 2 * odd).astype(F32) * nz
     lo_near, lo_far = (1 - odd) * (planes - reach), odd * (planes - reach)
-    ahead = planes - 2 * (HALO - REACH) - nz
-    deposit(pk_ref, 0, HALO - REACH, ahead, False)
+    out_near, out_far = (1 - odd) * (planes - 1), odd * (planes - 1)
+    reached = nz + 2 * REACH
+    ahead = 4
+    deposit(pk_ref, 0, HALO - REACH, ahead, False, OWN_WIDE)
     pl.semaphore_wait(barrier, count - 1)
     for c in near_copies:
         c.start()
@@ -252,7 +263,7 @@
         c.wait()
     start_y(den_y)
     start_y(p_y)
-    deposit(pk_ref, 0, HALO - REACH + ahead, nz, False)
+    deposit(pk_ref, 0, HALO - REACH + ahead, reached - ahead, False, OWN_WIDE)
 
     def tile_pair_of(i):
         return (
@@ -273,17 +284,20 @@
     prepare_all(near.at[0], side, 1)
     for i in range(reach, planes - reach):
         send_tiles(i)
-    deposit(near.at[0], 1, lo_near, reach - 4, True, None, send_tiles)
+    deposit(near.at[0], 1, out_near, 1, True, 1, None, send_tiles, 2)
+    early = reach - 1 - BESIDE
+    deposit(near.at[0], 1, lo_near + odd, early, True, NEAR_WIDE, None, send_tiles)
     near_copies[1].wait()
     start_z(den_z)
     start_z(p_z)
-    share = slots // (4 * (slots // CHUNK))
+    share = slots // (BESIDE // NEAR_WIDE * (slots // CHUNK))
 
     def prepare_far(n):
         prepare(near.at[1], -side, 2, n * share, share)
 
-    deposit(near.at[0], 1, lo_near + reach - 4, 4, True, prepare_far, send_tiles)
-    deposit(near.at[1], 2, lo_far, reach, True, None, send_tiles)
+    deposit(near.at[0], 1, lo_near + odd + early, BESIDE, True, NEAR_WIDE, prepare_far, send_tiles)
+    deposit(near.at[1], 2, out_far, 1, True, 1, None, send_tiles, 2)
+    deposit(near.at[1], 2, lo_far + 1 - odd, reach - 1, True, NEAR_WIDE, None, send_tiles)
 
     def add_tiles(lo, n):
         def body(j, carry):
@@ -298,57 +312,81 @@
             def _():
                 dep[i, :, ny : ny + EDGE, :] = dep[i, :, ny : ny + EDGE, :] + tile_in[1, i]
 
+            @pl.when(jnp.logical_not(has_s))
+            def _():
+                dep[i, :, HALO - 1 : HALO, :] = dep[i, :, HALO : HALO + 1, :]
+
+            @pl.when(jnp.logical_not(has_n))
+            def _():
+                dep[i, :, HALO + ny : HALO + ny + 1, :] = dep[i, :, HALO + ny - 1 : HALO + ny, :]
+
             return carry
 
         lax.fori_loop(0, n, body, 0)
 
-    def shifts_x(v):
+    def shifts_x(v, mirror=False):
         lane = lax.broadcasted_iota(jnp.int32, (v.shape[0], LANES), 1)
         parts = [v[:, at : at + LANES] for at in range(0, nx, LANES)]
         ups = [pltpu.roll(part, 1, 1) for part in parts]
         downs = [pltpu.roll(part, LANES - 1, 1) for part in parts]
-        west = [jnp.where(lane == 0, ups[n - 1] if n else 0.0, u) for n, u in enumerate(ups)]
+        first_wall, last_wall = (parts[0], parts[-1]) if mirror else (0.0, 0.0)
+        west = [jnp.where(lane == 0, ups[n - 1] if n else first_wall, u) for n, u in enumerate(ups)]
         east = [
-            jnp.where(lane == LANES - 1, downs[n + 1] if n + 1 < len(parts) else 0.0, u) for n, u in enumerate(downs)
+            jnp.where(lane == LANES - 1, downs[n + 1] if n + 1 < len(parts) else last_wall, u)
+            for n, u in enumerate(downs)
         ]
         return jnp.concatenate(west, axis=1), jnp.concatenate(east, axis=1)
 
-    def sweep(src, dst, lo, n):
-        place = lax.broadcasted_iota(jnp.int32, (rows, nx), 0) - HALO + first
-        lane = lax.broadcasted_iota(jnp.int32, (rows, nx), 1)
-        count = (
-            2.0
-            + (place >= 1).astype(F32)
-            + (place < total_y - 1).astype(F32)
-            + (lane >= 1).astype(F32)
-            + (lane < nx - 1).astype(F32)
-        )
-        inside = (place >= 0) & (place < total_y)
-        scale_c = jnp.where(inside, 1.0 - smooth_rate * count, 0.0)
-        scale_n = jnp.where(inside, smooth_rate, 0.0)
+    def sweep(src, dst, lo, n, last=False, ks=(0, 1, 2, 3)):
+        sub = lax.broadcasted_iota(jnp.int32, (8, nx), 0)
+        south_ghost = (sub == HALO - 1) & jnp.logical_not(has_s)
+        north_ghost = (sub == (HALO + ny) % 8) & jnp.logical_not(has_n)
 
         def body(j, carry):
             i = lo + j
-            for k in range(4):
-                c = src[i, k]
-                west, east = shifts_x(c)
-                beside = (
-                    src[i - 1, k] + src[i + 1, k] + pltpu.roll(c, 1, 0) + pltpu.roll(c, rows - 1, 0) + west + east
-                )
-                dst[i, k] = scale_c * c + scale_n * beside
+            for k in ks:
+
+                def turned(t):
+                    c = src[i, k, 8 * t : 8 * t + 8, :]
+                    return c, pltpu.roll(c, 1, 0), pltpu.roll(c, 7, 0)
+
+                lower, here = None, turned(0)
+                for t in range(rows // 8):
+                    upper = turned(t + 1) if t + 1 < rows // 8 else None
+                    c, south, north = here
+                    south = south if lower is None else jnp.where(sub == 0, lower[1], south)
+                    north = north if upper is None else jnp.where(sub == 7, upper[2], north)
+                    west, east = shifts_x(c, True)
+                    at = slice(8 * t, 8 * t + 8)
+                    beside = (src[i - 1, k, at, :] + src[i + 1, k, at, :]) + (south + north) + (west + east)
+                    out = (1.0 - 6.0 * smooth_rate) * c + smooth_rate * beside
+                    if t == 0:
+                        out = jnp.where(south_ghost, 0.0 if last else pltpu.roll(out, 7, 0), out)
+                    if upper is None:
+                        out = jnp.where(north_ghost, 0.0 if last else pltpu.roll(out, 1, 0), out)
+                    dst[i, k, at, :] = out
+                    lower, here = here, upper
             return carry
 
         lax.fori_loop(0, n, body, 0)
 
-    half = planes // 2 - 1
+    outer = (0, 1)
+    half = planes // 2 - 2
     bufs = [dep, fld]
     add_tiles(lo_near + (odd - 1) * (planes - 2 * reach), planes - reach)
-    sweep(dep, fld, 1 + (1 - odd) * half, half)
+    sweep(dep, fld, odd + (1 - odd) * (planes - 2), 1, False, outer)
+    sweep(dep, fld, 2 + (1 - odd) * half, half)
     add_tiles(lo_far, reach)
-    sweep(dep, fld, 1 + odd * half, half)
-    for s in range(1, SWEEPS):
-        sweep(bufs[s % 2], bufs[(s + 1) % 2], s + 1, planes - 2 * s - 2)
-    f = bufs[SWEEPS % 2]
+    sweep(dep, fld, 2 + odd * half, half)
+    sweep(dep, fld, (1 - odd) + odd * (planes - 2), 1, False, outer)
+    for s in range(1, SWEEPS - 1):
+        for edge_plane in (s + 1, planes - s - 2):
+            sweep(bufs[s % 2], bufs[(s + 1) % 2], edge_plane, 1, False, outer)
+        sweep(bufs[s % 2], bufs[(s + 1) % 2], s + 2, planes - 2 * s - 4)
+    before, f = bufs[(SWEEPS - 1) % 2], bufs[SWEEPS % 2]
+    for edge_plane, inner_plane in ((HALO - 1, HALO), (HALO + nz, HALO + nz - 2)):
+        sweep(before, f, edge_plane, 1, True, outer)
+        sweep(before, f, inner_plane, 2, True)
 
     def own(v, shift=0):
         return pltpu.roll(v, rows - HALO - shift, 0)[0:ny]
@@ -357,7 +395,7 @@
     wait_y(p_y)
     wait_z(den_z)
     wait_z(p_z)
-    for z in range(-1, nz + 1):
+    def mobility(z):
         g = own(1.0 / (1.0 + f[z + HALO, 0]))
         if 0 <= z < nz:
             gf_ref[z] = g
@@ -403,12 +441,11 @@
             slot, edge.at[slot - 2, 0], edge.at[slot - 2, 1], edge_in.at[slot - 2, 0], edge_in.at[slot - 2, 1]
         )
 
-    for z in range(nz + 1):
-        face_z[z] = 0.5 * (mob[z] + mob[z + 1])
-    order = [0, nz - 1] + list(range(1, nz - 1))
     inner_first = list(range(1, nz - 1)) + [0, nz - 1]
     z_z, w_z, z_y, w_y = pair_z(2, z_ref), pair_z(3, w_ref), edge_pair(2), edge_pair(3)
-    for z in order:
+    def source(z):
+        for side_z in (z, z + 1):
+            face_z[side_z] = 0.5 * (mob[side_z] + mob[side_z + 1])
         m = mob[z + 1]
         gs = f[z + HALO, 0, HALO - 1 : HALO, :]
         gn = f[z + HALO, 0, HALO + ny : HALO + ny + 1, :]
@@ -429,8 +466,17 @@
         z0 = r0 / dg
         z_ref[z] = z0
         keep_edge(0, z, z0)
-        if z == nz - 1:
-            start_z(z_z)
+
+    for z in (-1, 0, 1, nz - 2, nz - 1, nz):
+        mobility(z)
+    for z in (0, nz - 1):
+        source(z)
+    start_z(z_z)
+    sweep(before, f, HALO + 2, nz - 4, True)
+    for z in range(2, nz - 2):
+        mobility(z)
+    for z in range(1, nz - 1):
+        source(z)
     start_y(z_y)
 
     def fold(v):

time: 61.5 us -> 58.7 us (0.954)
  Pallas kernels: 59.9 us -> 57 us
    pallas_call x1, Pallas kernels: 58.3 us -> 55.3 us  [on_device(): pl.pallas_call(functools.partial(step_kernel, ngz, ngy, nz, ny, nx, slots...]
where the time goes in v1:
time: 58.7 us; the launch traced here: 58.4 us
  Pallas kernels  57 us (97%)
  between operations  1.45 us (2%)
    pallas_call x1, Pallas kernels, on_device(): pl.pallas_call(functools.partial(step_kernel, ngz, ngy, nz, ny, nx, slots...  55.3 us
    pallas_call x1, Pallas kernels, on_device(): pl.pallas_call(pass_kernel, out_shape=shapes, in_specs=[vmem] * 4, out_sp...  1.69 us

profile of v1, /device:TPU:0, one launch (start us, length us, event | category | flops | bytes accessed | tf_op | source)
XLA Modules:
  0.0 58.4 jit_solution(13610223396357694875)
XLA Ops:
  1.3 55.3 %shard_map.111 = (f32[8,64,256]{2,1,0:T(8,128)S(1)}, f32[8,3,64,256]{3,2,1,0:T(8,128)S(1)}, f32[8,64,256]{2,1,0:T(8,128)S(1)}, f32[8,64,256]{2,1,0:T(8,128)S(1)}) custom-call(s32[1,1]{1,0:T(1,128)S(6)} %copy.12.count_ref, s32[1,4096]{1,0:T(1,128)} %bitcast.2, f32[3,4096]{1,0:T(4,128)} %off_hbm.1, f32[1,4096]{1,0:T(1,128)} %bitcast.3, f32[3,4096]{1,0:T(4,128)} %force_hbm.1, ...), custom_call_target="tpu_custom_call" | custom-call | tf_op jit(solution)/shard_map/pallas_call | solution.py:567
  56.6 1.7 %shard_map.112 = (f32[8,64,256]{2,1,0:T(8,128)}, f32[8,3,64,256]{3,2,1,0:T(8,128)}, f32[8,64,256]{2,1,0:T(8,128)}, f32[8,64,256]{2,1,0:T(8,128)}) custom-call(f32[8,64,256]{2,1,0:T(8,128)S(1)} %get-tuple-element.8.refs_0_, f32[8,3,64,256]{3,2,1,0:T(8,128)S(1)} %get-tuple-element.9.refs_1_, f32[8,64,256]{2,1,0:T(8,128)S(1)} %get-tuple-element.10.refs_2_, ...), custom_call_target="tpu_custom_call" | custom-call | tf_op jit(solution)/shard_map/pallas_call | solution.py:609

commit v2 on v1

--- a/solution.py
+++ b/solution.py
@@ -16,7 +16,6 @@
 LANES = 128
 OWN_WIDE = 2
 NEAR_WIDE = 2
-BESIDE = 4
 smooth_rate = 0.15
 stiffness = 0.002
 F32 = jnp.float32
@@ -209,7 +208,7 @@
             for g in range(nx // 16):
                 wx_ref[slot, 16 * g : 16 * g + 16, sl] = jnp.where(block == g, v0, jnp.where(beside == g, v1, none))
 
-    def deposit(pk, slot, lo, n, add, wide=1, beside=None, after=None, parts=4):
+    def deposit(pk, slot, lo, n, add, wide=1, after=None, parts=4):
         assert n % wide == 0
 
         def body(j, carry):
@@ -227,8 +226,6 @@
                     lhs, wx_ref[slot, :, sl], (((1,), (1,)), ((), ())), preferred_element_type=F32
                 )
                 acc = part if acc is None else acc + part
-                if beside is not None:
-                    beside(j * (slots // CHUNK) + at // CHUNK)
             acc = acc.reshape(wide, parts, rows, nx)
             for h in range(wide):
                 dep[i + h, 0:parts] = dep[i + h, 0:parts] + acc[h] if add else acc[h]
@@ -284,20 +281,14 @@
     prepare_all(near.at[0], side, 1)
     for i in range(reach, planes - reach):
         send_tiles(i)
-    deposit(near.at[0], 1, out_near, 1, True, 1, None, send_tiles, 2)
-    early = reach - 1 - BESIDE
-    deposit(near.at[0], 1, lo_near + odd, early, True, NEAR_WIDE, None, send_tiles)
+    deposit(near.at[0], 1, out_near, 1, True, 1, send_tiles, 2)
+    deposit(near.at[0], 1, lo_near + odd, reach - 1, True, NEAR_WIDE, send_tiles)
     near_copies[1].wait()
     start_z(den_z)
     start_z(p_z)
-    share = slots // (BESIDE // NEAR_WIDE * (slots // CHUNK))
-
-    def prepare_far(n):
-        prepare(near.at[1], -side, 2, n * share, share)
-
-    deposit(near.at[0], 1, lo_near + odd + early, BESIDE, True, NEAR_WIDE, prepare_far, send_tiles)
-    deposit(near.at[1], 2, out_far, 1, True, 1, None, send_tiles, 2)
-    deposit(near.at[1], 2, lo_far + 1 - odd, reach - 1, True, NEAR_WIDE, None, send_tiles)
+    prepare_all(near.at[1], -side, 2)
+    deposit(near.at[1], 2, out_far, 1, True, 1, send_tiles, 2)
+    deposit(near.at[1], 2, lo_far + 1 - odd, reach - 1, True, NEAR_WIDE, send_tiles)
 
     def add_tiles(lo, n):
         def body(j, carry):

time: 58.7 us -> 57.9 us (0.986)
  Pallas kernels: 57 us -> 56.2 us
    pallas_call x1, Pallas kernels: 55.3 us -> 54.5 us  [on_device(): pl.pallas_call(functools.partial(step_kernel, ngz, ngy, nz, ny, nx, slots...]
where the time goes in v2:
time: 57.9 us; the launch traced here: 57.6 us
  Pallas kernels  56.2 us (97%)
  between operations  1.45 us (3%)
    pallas_call x1, Pallas kernels, on_device(): pl.pallas_call(functools.partial(step_kernel, ngz, ngy, nz, ny, nx, slots...  54.5 us
    pallas_call x1, Pallas kernels, on_device(): pl.pallas_call(pass_kernel, out_shape=shapes, in_specs=[vmem] * 4, out_sp...  1.69 us

profile of v2, /device:TPU:0, one launch (start us, length us, event | category | flops | bytes accessed | tf_op | source)
XLA Modules:
  0.0 57.6 jit_solution(10067575944320641078)
XLA Ops:
  1.3 54.5 %shard_map.111 = (f32[8,64,256]{2,1,0:T(8,128)S(1)}, f32[8,3,64,256]{3,2,1,0:T(8,128)S(1)}, f32[8,64,256]{2,1,0:T(8,128)S(1)}, f32[8,64,256]{2,1,0:T(8,128)S(1)}) custom-call(s32[1,1]{1,0:T(1,128)S(6)} %copy.12.count_ref, s32[1,4096]{1,0:T(1,128)} %bitcast.2, f32[3,4096]{1,0:T(4,128)} %off_hbm.1, f32[1,4096]{1,0:T(1,128)} %bitcast.3, f32[3,4096]{1,0:T(4,128)} %force_hbm.1, ...), custom_call_target="tpu_custom_call" | custom-call | tf_op jit(solution)/shard_map/pallas_call | solution.py:558
  55.7 1.7 %shard_map.112 = (f32[8,64,256]{2,1,0:T(8,128)}, f32[8,3,64,256]{3,2,1,0:T(8,128)}, f32[8,64,256]{2,1,0:T(8,128)}, f32[8,64,256]{2,1,0:T(8,128)}) custom-call(f32[8,64,256]{2,1,0:T(8,128)S(1)} %get-tuple-element.8.refs_0_, f32[8,3,64,256]{3,2,1,0:T(8,128)S(1)} %get-tuple-element.9.refs_1_, f32[8,64,256]{2,1,0:T(8,128)S(1)} %get-tuple-element.10.refs_2_, ...), custom_call_target="tpu_custom_call" | custom-call | tf_op jit(solution)/shard_map/pallas_call | solution.py:600
